TPU v7x, 256 devices: a whole 4x4x8 slice. The times are simulated.
256 devices in a mesh: dp: 2 (over core), expert: 128 (over z, x, y).
Axes of the slice: x: 4, y: 4, z: 8, core: 2. Of those that a mesh axis runs over, the one named last changes fastest.
Arguments:
- tokens: bfloat16 [32768, 2048], P(('dp', 'expert')), may hold values from -6 to 6
- out_grad: bfloat16 [32768, 2048], P(('dp', 'expert')), may hold values from -6 to 6
- expert_ids: int32 [32768, 4], P(('dp', 'expert')), may hold values from 0 to 127, as said below
- gate_weights: float32 [32768, 4], P(('dp', 'expert')), may hold values from 0.05 to 0.6
- w_in: bfloat16 [128, 2048, 768], P('expert'), may hold values from -0.125 to 0.125
- w_out: bfloat16 [128, 384, 2048], P('expert'), may hold values from -0.3125 to 0.3125
Outputs:
- token_grad: bfloat16 [32768, 2048], P(('dp', 'expert'))
- w_in_grad: bfloat16 [128, 2048, 768], P('expert', 'dp')
- w_out_grad: bfloat16 [128, 384, 2048], P('expert', None, 'dp')
Inputs may be any that keep to these rules, and one draw needn't show every extreme that they name: `expert_ids`: each token names 4 different experts; among the 128 tokens of one device no expert is named more than 7 times, and in every device's tokens some expert is named exactly 7 times.
All inputs are finite; a program needn't handle non-finite values.
Results may differ from a plain program's by a relative error of at most 0.0065.
Values may be sent and summed in bfloat16 or wider, within the bound.
No kernel may reach another device: no remote copies, remote signals or barrier semaphores. Data moves between devices by JAX's collectives and lax.ppermute only.
A program may use at most 128 MiB of HBM per device.

v0:
```python
import jax
import jax.numpy as jnp
from jax import lax
from jax.sharding import Mesh
from jax.sharding import PartitionSpec as P

Z, X, Y = (8, 4, 4)
PLANE = X * Y
CAP = 7
IN_CHUNKS = 1
GRAD_CHUNKS = 1
BACK_CHUNKS = 1
f32 = jnp.float32
bf16 = jnp.bfloat16


def mm(a, b, ca, cb):
    return lax.dot_general(a, b, (((ca,), (cb,)), ((), ())), preferred_element_type=f32)


def pieces(width, count):
    step = width // count
    return [(i * step, (i + 1) * step) for i in range(count)]


def silu_parts(gate_part):
    sigma = 1.0 / (1.0 + jnp.exp(-gate_part))
    return (gate_part * sigma, sigma * (1.0 + gate_part * (1.0 - sigma)))


def routing(meta, plane):
    sources, tok = (Z, meta.shape[-1])
    meta = meta.reshape(sources, 8, tok)
    ids = meta[:, :4].astype(jnp.int32)
    gates = meta[:, 4:]
    local = plane * PLANE + jnp.arange(PLANE, dtype=jnp.int32)
    match = ids[:, :, None, :] == local[None, None, :, None]
    named = jnp.any(match, axis=1)
    gate = jnp.sum(jnp.where(match, gates[:, :, None, :], 0.0), axis=1)
    index = jnp.arange(tok, dtype=jnp.int32)
    earlier = (index[:, None] < index[None, :]).astype(bf16)
    before = mm(named.astype(bf16).reshape(sources * PLANE, tok), earlier, 1, 0)
    rank = jnp.where(named, before.reshape(sources, PLANE, tok), -1.0)
    rank = rank.transpose(1, 0, 2)
    gate = gate.transpose(1, 0, 2)
    slot_rank = jnp.arange(CAP, dtype=jnp.int32).astype(f32)
    hit = rank[:, None] == slot_rank[None, :, None, None]
    slot_gate = jnp.sum(jnp.where(hit, gate[:, None], 0.0), axis=3).reshape(-1, 1)
    same = jnp.arange(sources)[:, None] == jnp.arange(sources)[None, :]
    wide = jnp.where(same[None, :, :, None], rank[:, None], -1.0).reshape(
        PLANE, 1, sources, sources * tok
    )
    slots = (wide == slot_rank[None, :, None, None]).astype(bf16)
    return (slots.reshape(PLANE * CAP * sources, sources * tok), slot_gate)


def body(tokens, out_grad, expert_ids, gate_weights, w_in, w_out):
    width = tokens.shape[1]
    w_in, w_out = (w_in[0], w_out[0])
    half = w_out.shape[0]
    plane = lax.axis_index("z")
    core = lax.axis_index("dp")

    def gather_z(x):
        return lax.all_gather(x, "z", axis=0, tiled=True)

    def swap_plane(x):
        return lax.all_to_all(x, ("x", "y"), split_axis=0, concat_axis=0, tiled=True)

    meta = gather_z(jnp.concatenate([expert_ids.astype(f32), gate_weights], axis=1).T)
    slots, slot_gate = routing(meta, plane)
    rows_in = []
    for lo, hi in pieces(width, IN_CHUNKS):
        every = gather_z(tokens[:, lo:hi])
        rows_in.append(swap_plane(mm(slots, every, 1, 0).astype(bf16)))
    rows_grad = []
    for lo, hi in pieces(width, GRAD_CHUNKS):
        every = gather_z(out_grad[:, lo:hi])
        rows_grad.append(swap_plane((mm(slots, every, 1, 0) * slot_gate).astype(bf16)))
    joined = sum(
        (mm(r, w_in[lo:hi], 1, 0) for r, (lo, hi) in zip(rows_in, pieces(width, IN_CHUNKS)))
    )
    d_hidden = sum(
        (mm(r, w_out[:, lo:hi], 1, 1) for r, (lo, hi) in zip(rows_grad, pieces(width, GRAD_CHUNKS)))
    )
    gate_part, up_part = (joined[:, :half], joined[:, half:])
    activated, derivative = silu_parts(gate_part)
    hidden = (activated * up_part).astype(bf16)
    d_joined = jnp.concatenate(
        [d_hidden * up_part * derivative, d_hidden * activated], axis=1
    ).astype(bf16)
    token_grad = []
    for lo, hi in pieces(width, BACK_CHUNKS):
        back = swap_plane(mm(d_joined, w_in[lo:hi], 1, 1).astype(bf16))
        part = mm(slots, back, 0, 0).astype(bf16)
        token_grad.append(lax.psum_scatter(part, "z", scatter_dimension=0, tiled=True))
    token_grad = jnp.concatenate(token_grad, axis=1)
    grad_in = mm(jnp.concatenate(rows_in, axis=1), d_joined, 0, 0)
    grad_out = mm(hidden, jnp.concatenate(rows_grad, axis=1), 0, 0)
    half_width = width // 2
    other = 1 - core

    def sum_cores(x, axis):
        keep = lax.dynamic_slice_in_dim(x, core * half_width, half_width, axis)
        send = lax.dynamic_slice_in_dim(x, other * half_width, half_width, axis)
        got = lax.ppermute(send, "dp", [(0, 1), (1, 0)])
        return (keep + got).astype(bf16)[None]

    return (token_grad, sum_cores(grad_in, 0), sum_cores(grad_out, 1))


def solution(mesh):
    split = Mesh(mesh.devices.reshape(2, Z, X, Y), ("dp", "z", "x", "y"))
    hosts = ("z", "x", "y")
    rows = P(("dp",) + hosts, None)
    in_specs = (rows, rows, rows, rows, P(hosts, None, None), P(hosts, None, None))
    out_specs = (rows, P(hosts, "dp", None), P(hosts, None, "dp"))
    return jax.shard_map(body, mesh=split, in_specs=in_specs, out_specs=out_specs, check_vma=False)
```

profile of v0, /device:TPU:1, one launch (start us, length us, event | category | flops | bytes accessed | tf_op | source)
XLA Modules:
  0.0 320.4 jit_solution(10744743611331638339)
XLA Ops:
  10.3 23.3 %all_gather.9 = f32[64,128]{1,0:T(8,128)S(1)} all-gather(f32[8,128]{1,0:T(8,128)S(1)} %maximum_bitcast_fusion), channel_id=1, replica_groups=mesh['dp'=2,'z'=8,'x'=4,'y'=4] {'z'}, dimensions={0}, use_global_device_ids=true | all-gather | bytes 36864 | tf_op jit(solution)/shard_map/all_gather | solution.py:65
  36.3 32.3 %all-gather.5.cloned.1.call-done = bf16[1024,2048]{1,0:T(8,128)(2,1)} async-done(((bf16[128,2048]{1,0:T(8,128)(2,1)}), bf16[1024,2048]{1,0:T(8,128)(2,1)}) %all-gather.5.cloned.1.call-update) | async-done | bytes 4194320 | tf_op jit(solution)/shard_map/all_gather | solution.py:65
  68.6 8.2 %convolution_convert_fusion.2 = bf16[896,2048]{1,0:T(8,128)(2,1)} fusion(pred[896,1024]{1,0:T(32,128)(4,1)} %bitcast_compare_fusion, bf16[1024,2048]{1,0:T(8,128)(2,1)} %all-gather.5.cloned.1.call-done), kind=kOutput, calls=%fused_computation.4 | convolution fusion | flops 3759931392 | bytes 8781824 | tf_op jit(solution)/shard_map/dot_general | solution.py:18
  76.8 6.6 %all-to-all-start.1 = ((bf16[16,56,2048]{2,1,0:T(8,128)(2,1)}), bf16[16,56,2048]{2,1,0:T(8,128)(2,1)}, u32[]{:S(2)}, u32[]{:S(2)}) async-start(bf16[16,56,2048]{2,1,0:T(8,128)(2,1)} %bitcast.52), calls=%async_computation.1 | async-start | bytes 7340032 | tf_op jit(solution)/shard_map/all_to_all | solution.py:68
  83.9 39.9 %all-gather.3.cloned.1.call-done = bf16[1024,2048]{1,0:T(8,128)(2,1)} async-done(((bf16[128,2048]{1,0:T(8,128)(2,1)}), bf16[1024,2048]{1,0:T(8,128)(2,1)}) %all-gather.3.cloned.1.call-update) | async-done | bytes 4194320 | tf_op jit(solution)/shard_map/all_gather | solution.py:65
  123.8 8.2 %multiply_convert_fusion = bf16[896,2048]{1,0:T(8,128)(2,1)} fusion(pred[896,1024]{1,0:T(32,128)(4,1)} %bitcast_compare_fusion, bf16[1024,2048]{1,0:T(8,128)(2,1)} %all-gather.3.cloned.1.call-done, f32[896]{0:T(1024)S(1)} %mul.43), kind=kOutput, calls=%fused_computation | convolution fusion | flops 3761766400 | bytes 8785408 | tf_op jit(solution)/shard_map/dot_general | solution.py:18
  132.8 11.7 %all-to-all-start = ((bf16[16,56,2048]{2,1,0:T(8,128)(2,1)}), bf16[16,56,2048]{2,1,0:T(8,128)(2,1)}, u32[]{:S(2)}, u32[]{:S(2)}) async-start(bf16[16,56,2048]{2,1,0:T(8,128)(2,1)} %bitcast.53), calls=%async_computation | async-start | bytes 7340032 | tf_op jit(solution)/shard_map/all_to_all | solution.py:68
  144.5 7.1 %fusion.1 = f32[896,768]{0,1:T(8,128)} fusion(bf16[896,2048]{1,0:T(8,128)(2,1)} %bitcast.11, bf16[1,2048,768]{2,1,0:T(8,128)(2,1)S(1)} %copy-done), kind=kOutput, calls=%fused_computation.6 | convolution fusion | flops 2818572288 | bytes 9568256 | tf_op jit(solution)/shard_map/dot_general | solution.py:18
  151.6 38.2 %all-to-all-done = bf16[16,56,2048]{2,1,0:T(8,128)(2,1)} async-done(((bf16[16,56,2048]{2,1,0:T(8,128)(2,1)}), bf16[16,56,2048]{2,1,0:T(8,128)(2,1)}, u32[]{:S(2)}, u32[]{:S(2)}) %all-to-all-start) | async-done | bytes 3670048 | tf_op jit(solution)/shard_map/all_to_all | solution.py:68
  189.8 5.4 %multiply_convert_fusion.3 = (bf16[896,384]{0,1:T(8,128)(2,1)S(1)}, bf16[896,384]{0,1:T(8,128)(2,1)S(1)}) fusion(f32[896,768]{0,1:T(8,128)} %fusion.1, bf16[896,2048]{1,0:T(8,128)(2,1)} %bitcast.8, bf16[1,384,2048]{2,1,0:T(8,128)(2,1)} %param.11), kind=kOutput, calls=%fused_computation.17 | convolution fusion | flops 1413758976 | bytes 9371648 | tf_op jit(solution)/shard_map/dot_general | solution.py:18
  195.2 4.6 %convolution_convert_fusion.1 = bf16[896,2048]{1,0:T(8,128)(2,1)} fusion(bf16[1,2048,768]{2,1,0:T(8,128)(2,1)S(1)} %copy-done, bf16[896,384]{0,1:T(8,128)(2,1)S(1)} %get-tuple-element.4, bf16[896,384]{0,1:T(8,128)(2,1)S(1)} %get-tuple-element.3), kind=kOutput, calls=%fused_computation.3 | convolution fusion | flops 2823159808 | bytes 8192000 | tf_op jit(solution)/shard_map/dot_general | solution.py:18
  199.8 4.6 %all-to-all-start.2 = ((bf16[16,56,2048]{2,1,0:T(8,128)(2,1)}), bf16[16,56,2048]{2,1,0:T(8,128)(2,1)}, u32[]{:S(2)}, u32[]{:S(2)}) async-start(bf16[16,56,2048]{2,1,0:T(8,128)(2,1)} %bitcast.54), calls=%async_computation.2 | async-start | bytes 7340032 | tf_op jit(solution)/shard_map/all_to_all | solution.py:68
  205.3 42.5 %all-to-all-done.2 = bf16[16,56,2048]{2,1,0:T(8,128)(2,1)} async-done(((bf16[16,56,2048]{2,1,0:T(8,128)(2,1)}), bf16[16,56,2048]{2,1,0:T(8,128)(2,1)}, u32[]{:S(2)}, u32[]{:S(2)}) %all-to-all-start.2) | async-done | bytes 3670048 | tf_op jit(solution)/shard_map/all_to_all | solution.py:68
  247.8 8.2 %convolution_convert_fusion = bf16[1024,2048]{1,0:T(8,128)(2,1)} fusion(pred[896,1024]{1,0:T(8,128)(4,1)S(1)} %bitcast.55, bf16[896,2048]{1,0:T(8,128)(2,1)} %bitcast.14), kind=kOutput, calls=%fused_computation.1 | convolution fusion | flops 3760193536 | bytes 8781824 | tf_op jit(solution)/shard_map/dot_general | solution.py:18
  257.3 5.6 %fusion.7 = f32[2048,768]{1,0:T(8,128)S(1)} fusion(bf16[896,2048]{1,0:T(8,128)(2,1)} %bitcast.11, bf16[896,384]{0,1:T(8,128)(2,1)S(1)} %copy-done.10, bf16[896,384]{0,1:T(8,128)(2,1)S(1)} %copy-done.8), kind=kOutput, calls=%fused_computation.21 | convolution fusion | flops 2821324800 | bytes 11337728 | tf_op jit(solution)/shard_map/dot_general | solution.py:18
  263.0 1.8 constant_dynamic-slice_fusion.1
  264.8 2.2 copy-done.2
  267.0 4.7 %collective-permute-start = (f32[1024,768]{1,0:T(8,128)}, f32[1024,768]{1,0:T(8,128)}, u32[]{:S(2)}, u32[]{:S(2)}) collective-permute-start(f32[1024,768]{1,0:T(8,128)} %constant_dynamic-slice_fusion.1), channel_id=1, source_target_pairs={{0,128},{128,0},{1,129},{129,1},{2,130},{130,2},{3,131},{131,3},{4... | collective-permute-start | bytes 9437192 | tf_op jit(solution)/shard_map/ppermute | solution.py:106
  271.7 3.9 %fusion.9 = f32[384,2048]{1,0:T(8,128)S(1)} fusion(bf16[896,2048]{1,0:T(8,128)(2,1)} %bitcast.8, f32[896,768]{0,1:T(8,128)S(1)} %copy-done.6), kind=kOutput, calls=%fused_computation.23 | convolution fusion | flops 1411350528 | bytes 9568256 | tf_op jit(solution)/shard_map/dot_general | solution.py:18
  275.6 1.8 copy-done.5
  278.7 3.7 %collective-permute-done.1 = f32[384,1024]{1,0:T(8,128)} collective-permute-done((f32[384,1024]{1,0:T(8,128)}, f32[384,1024]{1,0:T(8,128)}, u32[]{:S(2)}, u32[]{:S(2)}) %collective-permute-start.1) | collective-permute-done | bytes 1572896 | tf_op jit(solution)/shard_map/ppermute | solution.py:106
  282.4 3.2 fusion.8
  285.6 4.4 %fusion.3 = bf16[1,1024,768]{2,1,0:T(8,128)(2,1)} fusion(f32[1024,768]{1,0:T(8,128)} %collective-permute-done, f32[2048,768]{1,0:T(8,128)} %copy-done.2, s32[]{:T(128)S(6)} %select_n.37), kind=kLoop, calls=%fused_computation.10 | loop fusion | flops 1572864 | bytes 7864324 | tf_op jit(solution)/shard_map/broadcast_in_dim | solution.py:107
  290.0 23.9 %reduce-scatter.2.cloned.1.call-done = bf16[128,2048]{1,0:T(8,128)(2,1)} async-done(((bf16[1024,2048]{1,0:T(8,128)(2,1)}), bf16[128,2048]{1,0:T(8,128)(2,1)}) %reduce-scatter.2.cloned.1.call-update) | async-done | bytes 524304 | tf_op jit(solution)/shard_map/reduce_scatter | solution.py:96
  (51 shorter events, 10.4 us)
Async XLA Ops:
  7.2 137.4 %copy-start = (bf16[1,2048,768]{2,1,0:T(8,128)(2,1)S(1)}, bf16[1,2048,768]{2,1,0:T(8,128)(2,1)}, u32[]{:S(2)}) copy-start(bf16[1,2048,768]{2,1,0:T(8,128)(2,1)} %param.10) | copy-start | bytes 9437188
  7.2 61.4 %all-gather.5.cloned.1.call-start = ((), (), s32[]{:S(2)}) async-start(), calls=%async_computation.5 | async-start | bytes 4718592 | tf_op jit(solution)/shard_map/all_gather | solution.py:65
  7.9 115.9 %all-gather.3.cloned.1.call-start = ((), (), s32[]{:S(2)}) async-start(), calls=%async_computation.4 | async-start | bytes 4718592 | tf_op jit(solution)/shard_map/all_gather | solution.py:65
  34.0 0.8 copy-start.3
  76.8 56.0 %all-to-all-start.1 = ((bf16[16,56,2048]{2,1,0:T(8,128)(2,1)}), bf16[16,56,2048]{2,1,0:T(8,128)(2,1)}, u32[]{:S(2)}, u32[]{:S(2)}) async-start(bf16[16,56,2048]{2,1,0:T(8,128)(2,1)} %bitcast.52), calls=%async_computation.1 | async-start | bytes 7340032 | tf_op jit(solution)/shard_map/all_to_all | solution.py:68
  132.8 57.0 %all-to-all-start = ((bf16[16,56,2048]{2,1,0:T(8,128)(2,1)}), bf16[16,56,2048]{2,1,0:T(8,128)(2,1)}, u32[]{:S(2)}, u32[]{:S(2)}) async-start(bf16[16,56,2048]{2,1,0:T(8,128)(2,1)} %bitcast.53), calls=%async_computation | async-start | bytes 7340032 | tf_op jit(solution)/shard_map/all_to_all | solution.py:68
  195.2 4.6 %copy-start.7 = (bf16[896,384]{0,1:T(8,128)(2,1)}, bf16[896,384]{0,1:T(8,128)(2,1)S(1)}, u32[]{:S(2)}) copy-start(bf16[896,384]{0,1:T(8,128)(2,1)S(1)} %get-tuple-element.3) | copy-start | bytes 2064388
  195.2 4.6 %copy-start.9 = (bf16[896,384]{0,1:T(8,128)(2,1)}, bf16[896,384]{0,1:T(8,128)(2,1)S(1)}, u32[]{:S(2)}) copy-start(bf16[896,384]{0,1:T(8,128)(2,1)S(1)} %get-tuple-element.4) | copy-start | bytes 2064388
  199.8 4.9 %copy-start.4 = (f32[16,8,1024]{2,1,0:T(8,128)S(1)}, f32[16,8,1024]{2,1,0:T(8,128)}, u32[]{:S(2)}) copy-start(f32[16,8,1024]{2,1,0:T(8,128)} %copy-done.3) | copy-start | bytes 1572868
  199.8 48.0 %all-to-all-start.2 = ((bf16[16,56,2048]{2,1,0:T(8,128)(2,1)}), bf16[16,56,2048]{2,1,0:T(8,128)(2,1)}, u32[]{:S(2)}, u32[]{:S(2)}) async-start(bf16[16,56,2048]{2,1,0:T(8,128)(2,1)} %bitcast.54), calls=%async_computation.2 | async-start | bytes 7340032 | tf_op jit(solution)/shard_map/all_to_all | solution.py:68
  204.5 109.4 %reduce-scatter.2.cloned.1.call-start = ((), (), s32[]{:S(2)}) async-start(), calls=%async_computation.6 | async-start | bytes 4718592 | tf_op jit(solution)/shard_map/reduce_scatter | solution.py:96
  256.0 1.1 copy-start.8
  256.0 1.3 copy-start.10
  262.9 4.0 %copy-start.2 = (f32[2048,768]{1,0:T(8,128)}, f32[2048,768]{1,0:T(8,128)S(1)}, u32[]{:S(2)}) copy-start(f32[2048,768]{1,0:T(8,128)S(1)} %fusion.7) | copy-start | bytes 18874372
  263.0 8.7 %copy-start.6 = (f32[896,768]{0,1:T(8,128)S(1)}, f32[896,768]{0,1:T(8,128)}, u32[]{:S(2)}) copy-start(f32[896,768]{0,1:T(8,128)} %fusion.1) | copy-start | bytes 8257540
  267.0 18.6 %collective-permute-start = (f32[1024,768]{1,0:T(8,128)}, f32[1024,768]{1,0:T(8,128)}, u32[]{:S(2)}, u32[]{:S(2)}) collective-permute-start(f32[1024,768]{1,0:T(8,128)} %constant_dynamic-slice_fusion.1), channel_id=1, source_target_pairs={{0,128},{128,0},{1,129},{129,1},{2,130},{130,2},{3,131},{131,3},{4... | collective-permute-start | bytes 9437192 | tf_op jit(solution)/shard_map/ppermute | solution.py:106
  275.6 1.8 copy-start.5
  278.7 3.8 %collective-permute-start.1 = (f32[384,1024]{1,0:T(8,128)}, f32[384,1024]{1,0:T(8,128)}, u32[]{:S(2)}, u32[]{:S(2)}) collective-permute-start(f32[384,1024]{1,0:T(8,128)} %constant_dynamic-slice_fusion), channel_id=1, source_target_pairs={{0,128},{128,0},{1,129},{129,1},{2,130},{130,2},{3,131},{131,3},{4... | collective-permute-start | bytes 4718600 | tf_op jit(solution)/shard_map/ppermute | solution.py:106
  282.4 31.4 %copy-start.1 = (bf16[1,2048,768]{2,1,0:T(8,128)(2,1)S(1)}, bf16[1,2048,768]{2,1,0:T(8,128)(2,1)}, u32[]{:S(2)}) copy-start(bf16[1,2048,768]{2,1,0:T(8,128)(2,1)} %param.10) | copy-start | bytes 9437188
Sparse Core Ops, SparseCore 0:
  9.8 58.7 all-gather.4
  70.4 53.4 all-gather.2
  256.2 57.6 reduce-scatter.1
where the time goes:
time: 321 us; the launch traced here: 320 us
  waiting for transfers between devices  183 us (57%)
  matrix products  51.4 us (16%)
  starting transfers between devices  28 us (9%)
  blocking collectives  23.3 us (7%)
  between operations  14 us (4%)
  other arithmetic  11.5 us (4%)
  local copies, waits for them, and re-layouts  9.6 us (3%)
    all_to_all x3, waiting for transfers between devices, swap_plane(): lax.all_to_all(x, ('x', 'y'), split_axis=0, concat_axis=0, tiled=True)  81.4 us
    all_gather x2, waiting for transfers between devices, gather_z(): return lax.all_gather(x, 'z', axis=0, tiled=True)  72.2 us
    dot_general x9, matrix products, mm(): lax.dot_general(a, b, (((ca,), (cb,)), ((), ())), preferred_element_type=...  51.4 us
    reduce_scatter x1, waiting for transfers between devices, body(): lax.psum_scatter(part, 'z', scatter_dimension=0, tiled=True)  23.9 us
    all_gather x1, blocking collectives, gather_z(): return lax.all_gather(x, 'z', axis=0, tiled=True)  23.3 us
    all_to_all x3, starting transfers between devices, swap_plane(): lax.all_to_all(x, ('x', 'y'), split_axis=0, concat_axis=0, tiled=True)  23 us
    broadcast_in_dim x2, other arithmetic, sum_cores(): return (keep + got).astype(bf16)[None]  7.52 us
  transfers between devices with their start and end apart: 8, of which 7 were waited for; matrix products, arithmetic and copies ran while one was open for 15% of the time, Pallas kernels for 0%

commit v1 on v0

--- a/solution.py
+++ b/solution.py
@@ -62,7 +62,9 @@
     core = lax.axis_index("dp")
 
     def gather_z(x):
-        return lax.all_gather(x, "z", axis=0, tiled=True)
+        return jnp.concatenate(
+            lax.all_to_all(jnp.stack([x] * lax.axis_size("z")), "z", 0, 0), axis=0
+        )
 
     def swap_plane(x):
         return lax.all_to_all(x, ("x", "y"), split_axis=0, concat_axis=0, tiled=True)

time: 321 us -> 451 us (1.40)
  blocking collectives: 23.3 us -> 165 us
  waiting for transfers between devices: 183 us -> 173 us
    all_to_all x0 -> x3, blocking collectives: none -> 165 us  [the longest x2 112 us: gather_z(): lax.all_to_all(jnp.stack([x] * lax.axis_size('z')), 'z', 0, 0)]
    all_to_all x0 -> x1, waiting for transfers between devices: none -> 81.6 us  [gather_z(): lax.all_to_all(jnp.stack([x] * lax.axis_size('z')), 'z', 0, 0)]
    all_gather x2 -> x0, waiting for transfers between devices: 72.2 us -> none  [gather_z(): return lax.all_gather(x, 'z', axis=0, tiled=True)]
    all_gather x1 -> x0, blocking collectives: 23.3 us -> none  [gather_z(): return lax.all_gather(x, 'z', axis=0, tiled=True)]
    all_to_all x3 -> x2, waiting for transfers between devices: 81.4 us -> 62.3 us  [swap_plane(): lax.all_to_all(x, ('x', 'y'), split_axis=0, concat_axis=0, tiled=True)]
    all_to_all x3 -> x2, starting transfers between devices: 23 us -> 16.3 us  [swap_plane(): lax.all_to_all(x, ('x', 'y'), split_axis=0, concat_axis=0, tiled=True)]
    all_to_all x0 -> x1, starting transfers between devices: none -> 4.55 us  [gather_z(): lax.all_to_all(jnp.stack([x] * lax.axis_size('z')), 'z', 0, 0)]
  transfers between devices with their start and end apart: 8 -> 6, of which waited for: 7 -> 5; matrix products, arithmetic and copies ran while one was open for 15% -> 10% of each run, Pallas kernels for 0% -> 0%
where the time goes in v1:
time: 451 us; the launch traced here: 450 us
  waiting for transfers between devices  173 us (38%)
  blocking collectives  165 us (37%)
  matrix products  47.5 us (11%)
  starting transfers between devices  27.4 us (6%)
  between operations  14.3 us (3%)
  local copies, waits for them, and re-layouts  13.6 us (3%)
  other arithmetic  10.3 us (2%)
    all_to_all x2, blocking collectives, gather_z(): lax.all_to_all(jnp.stack([x] * lax.axis_size('z')), 'z', 0, 0)  112 us
    all_to_all x1, waiting for transfers between devices, gather_z(): lax.all_to_all(jnp.stack([x] * lax.axis_size('z')), 'z', 0, 0)  81.6 us
    all_to_all x2, waiting for transfers between devices, swap_plane(): lax.all_to_all(x, ('x', 'y'), split_axis=0, concat_axis=0, tiled=True)  62.3 us
    all_to_all x1, blocking collectives, swap_plane(): lax.all_to_all(x, ('x', 'y'), split_axis=0, concat_axis=0, tiled=True)  52.3 us
    dot_general x9, matrix products, mm(): lax.dot_general(a, b, (((ca,), (cb,)), ((), ())), preferred_element_type=...  47.5 us
    reduce_scatter x1, waiting for transfers between devices, body(): lax.psum_scatter(part, 'z', scatter_dimension=0, tiled=True)  25.2 us
    all_to_all x2, starting transfers between devices, swap_plane(): lax.all_to_all(x, ('x', 'y'), split_axis=0, concat_axis=0, tiled=True)  16.3 us
  transfers between devices with their start and end apart: 6, of which 5 were waited for; matrix products, arithmetic and copies ran while one was open for 10% of the time, Pallas kernels for 0%

profile of v1, /device:TPU:1, one launch (start us, length us, event | category | flops | bytes accessed | tf_op | source)
XLA Modules:
  0.0 450.4 jit_solution(3490570285598767060)
XLA Ops:
  8.8 15.7 %all_to_all.51 = f32[8,8,128]{2,1,0:T(8,128)S(1)} all-to-all(f32[8,8,128]{2,1,0:T(8,128)S(1)} %stack.6), channel_id=1, replica_groups=mesh['dp'=2,'z'=8,'x'=4,'y'=4] {'z'}, dimensions={0} | all-to-all | bytes 65536 | tf_op jit(solution)/shard_map/all_to_all | solution.py:66
  26.1 96.6 %all_to_all.52 = bf16[8,128,2048]{2,1,0:T(8,128)(2,1)} all-to-all(bf16[8,128,2048]{2,1,0:T(8,128)(2,1)S(1)} %stack.8), channel_id=1, replica_groups=mesh['dp'=2,'z'=8,'x'=4,'y'=4] {'z'}, dimensions={0} | all-to-all | bytes 8388608 | tf_op jit(solution)/shard_map/all_to_all | solution.py:66
  122.7 2.5 stack.7
  125.2 4.6 %all-to-all-start.1 = ((bf16[8,128,2048]{2,1,0:T(8,128)(2,1)}), bf16[8,128,2048]{2,1,0:T(8,128)(2,1)}, u32[]{:S(2)}, u32[]{:S(2)}) async-start(bf16[8,128,2048]{2,1,0:T(8,128)(2,1)} %stack.7), calls=%async_computation.1 | async-start | bytes 8388608 | tf_op jit(solution)/shard_map/all_to_all | solution.py:66
  131.7 7.6 %convolution_convert_fusion.2 = bf16[896,2048]{1,0:T(8,128)(2,1)} fusion(pred[896,1024]{1,0:T(8,128)(4,1)S(1)} %bitcast.56, bf16[1024,2048]{1,0:T(8,128)(2,1)} %bitcast.51), kind=kOutput, calls=%fused_computation.3 | convolution fusion | flops 3759931392 | bytes 8781824 | tf_op jit(solution)/shard_map/dot_general | solution.py:18
  139.3 81.6 %all-to-all-done.1 = bf16[8,128,2048]{2,1,0:T(8,128)(2,1)} async-done(((bf16[8,128,2048]{2,1,0:T(8,128)(2,1)}), bf16[8,128,2048]{2,1,0:T(8,128)(2,1)}, u32[]{:S(2)}, u32[]{:S(2)}) %all-to-all-start.1) | async-done | bytes 4194336 | tf_op jit(solution)/shard_map/all_to_all | solution.py:66
  220.9 6.8 %all-to-all-start.4 = ((bf16[16,56,2048]{2,1,0:T(8,128)(2,1)}), bf16[16,56,2048]{2,1,0:T(8,128)(2,1)}, u32[]{:S(2)}, u32[]{:S(2)}) async-start(bf16[16,56,2048]{2,1,0:T(8,128)(2,1)} %bitcast.52), calls=%async_computation.4 | async-start | bytes 7340032 | tf_op jit(solution)/shard_map/all_to_all | solution.py:70
  228.2 8.2 %multiply_convert_fusion = bf16[896,2048]{1,0:T(8,128)(2,1)} fusion(pred[896,1024]{1,0:T(8,128)(4,1)} %bitcast.57, bf16[1024,2048]{1,0:T(8,128)(2,1)} %bitcast.4, f32[896]{0:T(1024)S(1)} %mul.43), kind=kOutput, calls=%fused_computation | convolution fusion | flops 3761766400 | bytes 8785408 | tf_op jit(solution)/shard_map/dot_general | solution.py:18
  236.4 31.8 %all-to-all-done.4 = bf16[16,56,2048]{2,1,0:T(8,128)(2,1)} async-done(((bf16[16,56,2048]{2,1,0:T(8,128)(2,1)}), bf16[16,56,2048]{2,1,0:T(8,128)(2,1)}, u32[]{:S(2)}, u32[]{:S(2)}) %all-to-all-start.4) | async-done | bytes 3670048 | tf_op jit(solution)/shard_map/all_to_all | solution.py:70
  268.2 9.5 %all-to-all-start.2 = ((bf16[16,56,2048]{2,1,0:T(8,128)(2,1)}), bf16[16,56,2048]{2,1,0:T(8,128)(2,1)}, u32[]{:S(2)}, u32[]{:S(2)}) async-start(bf16[16,56,2048]{2,1,0:T(8,128)(2,1)} %bitcast.53), calls=%async_computation.2 | async-start | bytes 7340032 | tf_op jit(solution)/shard_map/all_to_all | solution.py:70
  277.9 7.0 %fusion.1 = f32[896,768]{0,1:T(8,128)} fusion(bf16[896,2048]{1,0:T(8,128)(2,1)} %bitcast.11, bf16[1,2048,768]{2,1,0:T(8,128)(2,1)S(1)} %copy-done), kind=kOutput, calls=%fused_computation.5 | convolution fusion | flops 2818572288 | bytes 9568256 | tf_op jit(solution)/shard_map/dot_general | solution.py:18
  285.0 30.5 %all-to-all-done.2 = bf16[16,56,2048]{2,1,0:T(8,128)(2,1)} async-done(((bf16[16,56,2048]{2,1,0:T(8,128)(2,1)}), bf16[16,56,2048]{2,1,0:T(8,128)(2,1)}, u32[]{:S(2)}, u32[]{:S(2)}) %all-to-all-start.2) | async-done | bytes 3670048 | tf_op jit(solution)/shard_map/all_to_all | solution.py:70
  315.5 5.4 %multiply_convert_fusion.3 = (bf16[896,384]{0,1:T(8,128)(2,1)S(1)}, bf16[896,384]{0,1:T(8,128)(2,1)S(1)}) fusion(f32[896,768]{0,1:T(8,128)} %fusion.1, bf16[896,2048]{1,0:T(8,128)(2,1)} %bitcast.7, bf16[1,384,2048]{2,1,0:T(8,128)(2,1)} %param.11), kind=kOutput, calls=%fused_computation.16 | convolution fusion | flops 1413758976 | bytes 9371648 | tf_op jit(solution)/shard_map/dot_general | solution.py:18
  320.9 3.3 convolution_convert_fusion.1
  324.3 52.3 %all_to_all.53 = bf16[16,56,2048]{2,1,0:T(8,128)(2,1)S(1)} all-to-all(bf16[16,56,2048]{2,1,0:T(8,128)(2,1)S(1)} %bitcast.55), channel_id=1, replica_groups=mesh['dp'=2,'z'=8,'x'=4,'y'=4] {'x','y'}, dimensions={0} | all-to-all | bytes 7340032 | tf_op jit(solution)/shard_map/all_to_all | solution.py:70
  376.6 6.3 %convolution_convert_fusion = bf16[1024,2048]{1,0:T(8,128)(2,1)} fusion(pred[896,1024]{1,0:T(8,128)(4,1)S(1)} %bitcast.58, bf16[896,2048]{1,0:T(8,128)(2,1)S(1)} %bitcast.54), kind=kOutput, calls=%fused_computation.1 | convolution fusion | flops 3760193536 | bytes 8781824 | tf_op jit(solution)/shard_map/dot_general | solution.py:18
  384.2 5.6 %fusion.7 = f32[2048,768]{1,0:T(8,128)S(1)} fusion(bf16[896,2048]{1,0:T(8,128)(2,1)} %bitcast.11, bf16[896,384]{0,1:T(8,128)(2,1)S(1)} %copy-done.11, bf16[896,384]{0,1:T(8,128)(2,1)S(1)} %copy-done.9), kind=kOutput, calls=%fused_computation.20 | convolution fusion | flops 2821324800 | bytes 11337728 | tf_op jit(solution)/shard_map/dot_general | solution.py:18
  391.7 2.1 copy-done.2
  393.9 6.2 %collective-permute-start = (f32[1024,768]{1,0:T(8,128)}, f32[1024,768]{1,0:T(8,128)}, u32[]{:S(2)}, u32[]{:S(2)}) collective-permute-start(f32[1024,768]{1,0:T(8,128)} %constant_dynamic-slice_fusion.1), channel_id=1, source_target_pairs={{0,128},{128,0},{1,129},{129,1},{2,130},{130,2},{3,131},{131,3},{4... | collective-permute-start | bytes 9437192 | tf_op jit(solution)/shard_map/ppermute | solution.py:108
  400.1 3.9 fusion.9
  407.3 3.6 collective-permute-done.1
  410.9 3.2 fusion.8
  414.0 4.3 fusion.3
  418.4 25.2 %reduce-scatter.2.cloned.1.call-done = bf16[128,2048]{1,0:T(8,128)(2,1)} async-done(((bf16[1024,2048]{1,0:T(8,128)(2,1)}), bf16[128,2048]{1,0:T(8,128)(2,1)}) %reduce-scatter.2.cloned.1.call-update) | async-done | bytes 524304 | tf_op jit(solution)/shard_map/reduce_scatter | solution.py:98
  (49 shorter events, 12.3 us)
Async XLA Ops:
  7.2 270.8 %copy-start = (bf16[1,2048,768]{2,1,0:T(8,128)(2,1)S(1)}, bf16[1,2048,768]{2,1,0:T(8,128)(2,1)}, u32[]{:S(2)}) copy-start(bf16[1,2048,768]{2,1,0:T(8,128)(2,1)} %param.10) | copy-start | bytes 9437188
  26.1 96.6 %copy-start.6 = (bf16[128,2048]{1,0:T(8,128)(2,1)S(1)}, bf16[128,2048]{1,0:T(8,128)(2,1)}, u32[]{:S(2)}) copy-start(bf16[128,2048]{1,0:T(8,128)(2,1)} %param.7) | copy-start | bytes 1572868
  125.2 95.7 %all-to-all-start.1 = ((bf16[8,128,2048]{2,1,0:T(8,128)(2,1)}), bf16[8,128,2048]{2,1,0:T(8,128)(2,1)}, u32[]{:S(2)}, u32[]{:S(2)}) async-start(bf16[8,128,2048]{2,1,0:T(8,128)(2,1)} %stack.7), calls=%async_computation.1 | async-start | bytes 8388608 | tf_op jit(solution)/shard_map/all_to_all | solution.py:66
  130.8 0.9 copy-start.4
  220.9 47.3 %all-to-all-start.4 = ((bf16[16,56,2048]{2,1,0:T(8,128)(2,1)}), bf16[16,56,2048]{2,1,0:T(8,128)(2,1)}, u32[]{:S(2)}, u32[]{:S(2)}) async-start(bf16[16,56,2048]{2,1,0:T(8,128)(2,1)} %bitcast.52), calls=%async_computation.4 | async-start | bytes 7340032 | tf_op jit(solution)/shard_map/all_to_all | solution.py:70
  268.2 47.3 %all-to-all-start.2 = ((bf16[16,56,2048]{2,1,0:T(8,128)(2,1)}), bf16[16,56,2048]{2,1,0:T(8,128)(2,1)}, u32[]{:S(2)}, u32[]{:S(2)}) async-start(bf16[16,56,2048]{2,1,0:T(8,128)(2,1)} %bitcast.53), calls=%async_computation.2 | async-start | bytes 7340032 | tf_op jit(solution)/shard_map/all_to_all | solution.py:70
  277.7 165.8 %reduce-scatter.2.cloned.1.call-start = ((), (), s32[]{:S(2)}) async-start(), calls=%async_computation.7 | async-start | bytes 4718592 | tf_op jit(solution)/shard_map/reduce_scatter | solution.py:98
  320.9 3.4 copy-start.8
  320.9 3.4 copy-start.10
  324.3 52.3 %copy-start.5 = (pred[16,7,8,1024]{3,2,1,0:T(8,128)(4,1)S(1)}, pred[16,7,8,1024]{3,2,1,0:T(8,128)(4,1)}, u32[]{:S(2)}) copy-start(pred[16,7,8,1024]{3,2,1,0:T(8,128)(4,1)} %copy-done.4) | copy-start | bytes 2752516
  382.9 1.1 copy-start.9
  382.9 1.3 copy-start.11
  389.8 4.0 copy-start.2
  389.8 10.2 %copy-start.7 = (f32[896,768]{0,1:T(8,128)S(1)}, f32[896,768]{0,1:T(8,128)}, u32[]{:S(2)}) copy-start(f32[896,768]{0,1:T(8,128)} %fusion.1) | copy-start | bytes 8257540
  393.9 20.1 %collective-permute-start = (f32[1024,768]{1,0:T(8,128)}, f32[1024,768]{1,0:T(8,128)}, u32[]{:S(2)}, u32[]{:S(2)}) collective-permute-start(f32[1024,768]{1,0:T(8,128)} %constant_dynamic-slice_fusion.1), channel_id=1, source_target_pairs={{0,128},{128,0},{1,129},{129,1},{2,130},{130,2},{3,131},{131,3},{4... | collective-permute-start | bytes 9437192 | tf_op jit(solution)/shard_map/ppermute | solution.py:108
  404.0 1.8 copy-start.3
  407.1 3.8 collective-permute-start.1
  410.8 32.7 %copy-start.1 = (bf16[1,2048,768]{2,1,0:T(8,128)(2,1)S(1)}, bf16[1,2048,768]{2,1,0:T(8,128)(2,1)}, u32[]{:S(2)}) copy-start(bf16[1,2048,768]{2,1,0:T(8,128)(2,1)} %param.10) | copy-start | bytes 9437188
Sparse Core Ops, SparseCore 0:
  383.1 60.4 reduce-scatter.1
